TPU v7x, 32 devices: a whole 2x2x4 slice. The times are simulated.
32 devices in a mesh: groups: 2 (over y), atoms: 8 (over z, x), samples: 2 (over core).
Axes of the slice: x: 2, y: 2, z: 4, core: 2. Of those that a mesh axis runs over, the one named last changes fastest.
Arguments:
- act: bfloat16 [16, 10240, 128], P('samples', ('groups', 'atoms')), parts along dimension 1, may hold values from -6 to 6
- grad_out: bfloat16 [16, 10240, 128], P('samples', ('groups', 'atoms')), parts along dimension 1, may hold values from -6 to 6
- pair: bfloat16 [320, 32, 16, 128], P(('groups', 'atoms')), parts along dimension 0, may hold values from -500 to 500
- w_query: bfloat16 [128, 128], replicated, may hold values from -0.5 to 0.5
- w_key: bfloat16 [128, 128], replicated, may hold values from -0.5 to 0.5
- w_value: bfloat16 [128, 128], replicated, may hold values from -0.5 to 0.5
- w_gate: bfloat16 [128, 128], replicated, may hold values from -0.5 to 0.5
- w_out: bfloat16 [128, 128], replicated, may hold values from -0.5 to 0.5
- w_pair: bfloat16 [16, 4], replicated, may hold values from -1.5 to 1.5
- w_token: float32 [4], replicated, may hold values from -2 to 2
- offsets: int32 [320], P(('groups', 'atoms')), parts along dimension 0, may hold values from -128 to 32, as said below
- atom_token: int32 [10240], P(('groups', 'atoms')), parts along dimension 0, may hold values from 0 to 639, never falling along the last dimension, each value on 1 to 24 neighbouring positions
- padding: int32 [16], P(('groups', 'atoms')), parts along dimension 0, may hold values from 0 to 64, as said below
Outputs:
- grad_act: bfloat16 [16, 10240, 128], P('samples', ('groups', 'atoms')), parts along dimension 1
- grad_pair: bfloat16 [320, 32, 16, 128], P(('groups', 'atoms'), 'samples'), parts along dimension 0
- grad_weights: float32 [10, 128, 128], P('groups'), parts along dimension 0
- grad_pair_weight: float32 [32, 4], P('groups'), parts along dimension 0
- grad_token_weight: float32 [8], P('groups'), parts along dimension 0
There are 2 independent parts, one for each index of `groups`. A program takes and returns all parts, laid end to end along the dimension named above; an argument that names none is the same for every part. Nothing has to cross between parts.
Inputs may be any that keep to these rules, and one draw needn't show every extreme that they name: Window w reads the 128 atoms that begin at 32 * w + offsets[w], moved into the complex. padding[r] atoms at the end of atom range r are padding. `atom_token`: the atoms of one token are contiguous, at most 24 of them.
All inputs are finite; a program needn't handle non-finite values.
Results may differ from a plain program's by a relative error of at most 0.025.
Values may be sent and summed in bfloat16 or wider, within the bound.
A program may use at most 128 MiB of HBM per device.

v0:
```python
import math
import jax
import jax.numpy as jnp
from jax import lax
from jax.sharding import PartitionSpec as P

MASKED = -1000000000.0


def with_halo(value, sides, width):
    for axis, dim in sides:
        count, length = (lax.axis_size(axis), value.shape[dim])
        up = [(i, (i + 1) % count) for i in range(count - 1)]
        down = [(j, i) for i, j in up]
        last = lax.slice_in_dim(value, length - width, length, axis=dim)
        initial = lax.slice_in_dim(value, 0, width, axis=dim)
        before = lax.ppermute(last, axis, up)
        after = lax.ppermute(initial, axis, down)
        value = jnp.concatenate([before, value, after], axis=dim)
    return value


def passed_along(value, axis, steps):
    count = lax.axis_size(axis)
    initial, last = (max(0, -steps), min(count, count - steps))
    return lax.ppermute(value, axis, [(source, source + steps) for source in range(initial, last)])


def attend(query, keys, values, gate_logit, grad_y, pair_bias, key_live):
    windows = keys.shape[0]
    head_count = pair_bias.shape[1]
    channels = query.shape[-1]
    head_dim = channels // head_count
    score_scale = 1.0 / math.sqrt(head_dim)
    query_heads = query.reshape(windows, -1, head_count, head_dim)
    key_heads = keys.reshape(windows, -1, head_count, head_dim)
    value_heads = values.reshape(windows, -1, head_count, head_dim)
    scores = (
        jnp.einsum("wihd,wjhd->whij", query_heads, key_heads, preferred_element_type=jnp.float32)
        * score_scale
        + pair_bias
    )
    scores = jnp.where(key_live[:, None, None, :], scores, MASKED)
    row_max = jnp.max(scores, axis=-1, keepdims=True)
    exponent = jnp.exp(scores - row_max)
    attn_probs = exponent / jnp.sum(exponent, axis=-1, keepdims=True)
    probs_b = attn_probs.astype(jnp.bfloat16)
    attended = jnp.einsum(
        "whij,wjhd->wihd", probs_b, value_heads, preferred_element_type=jnp.float32
    ).reshape(query.shape)
    gate_value = jax.nn.sigmoid(gate_logit)
    gated = (gate_value * attended).astype(jnp.bfloat16)
    d_attended = (grad_y * gate_value).astype(jnp.bfloat16)
    d_gate = (grad_y * attended * gate_value * (1.0 - gate_value)).astype(jnp.bfloat16)
    attended_heads = d_attended.reshape(windows, -1, head_count, head_dim)
    d_probs = jnp.einsum(
        "wihd,wjhd->whij", attended_heads, value_heads, preferred_element_type=jnp.float32
    )
    d_scores = attn_probs * (d_probs - jnp.sum(attn_probs * d_probs, axis=-1, keepdims=True))
    ds_b = d_scores.astype(jnp.bfloat16)
    d_query = (
        (
            jnp.einsum("whij,wjhd->wihd", ds_b, key_heads, preferred_element_type=jnp.float32)
            * score_scale
        )
        .astype(jnp.bfloat16)
        .reshape(query.shape)
    )
    d_keys = (
        jnp.einsum("whij,wihd->wjhd", ds_b, query_heads, preferred_element_type=jnp.float32)
        * score_scale
    )
    d_values = jnp.einsum(
        "whij,wihd->wjhd", probs_b, attended_heads, preferred_element_type=jnp.float32
    )
    return (gated, d_query, d_gate, d_keys, d_values, d_scores)


def per_device(
    act,
    grad_out,
    pair,
    w_query,
    w_key,
    w_value,
    w_gate,
    w_out,
    w_pair,
    w_token,
    offsets,
    atom_token,
    padding,
):
    sample_count, atom_count, channels = act.shape
    windows = offsets.shape[0]
    win_rows = atom_count // windows
    key_span = pair.shape[-1]
    ranges = lax.axis_size("atoms")
    anchor = lax.axis_index("atoms") * atom_count
    position = jnp.arange(atom_count, dtype=jnp.int32)
    is_live = position < atom_count - padding[0]
    atom_codes = jnp.where(is_live, atom_token + 1, 0)
    wide_codes = with_halo(atom_codes, (("atoms", 0),), key_span)
    starts = jnp.clip(
        anchor + win_rows * jnp.arange(windows, dtype=jnp.int32) + offsets,
        0,
        ranges * atom_count - key_span,
    )
    key_rows = starts[:, None] - anchor + key_span + jnp.arange(key_span, dtype=jnp.int32)[None, :]
    key_codes = wide_codes[key_rows]
    key_live = key_codes > 0
    same_token = key_codes[:, None, :] == (atom_token + 1).reshape(windows, win_rows)[:, :, None]
    pair_bias = jnp.einsum(
        "wicj,ch->whij", pair, w_pair, preferred_element_type=jnp.float32
    ) + w_token[None, :, None, None] * same_token[:, None, :, :].astype(jnp.float32)
    projection = jnp.concatenate([w_query, w_key, w_value, w_gate], axis=1)
    flat_act = act.reshape(sample_count * atom_count, channels)
    mixed = jnp.dot(flat_act, projection, preferred_element_type=jnp.float32).reshape(
        sample_count, atom_count, 4 * channels
    )
    query = mixed[..., :channels].astype(jnp.bfloat16)
    key_value = mixed[..., channels : 3 * channels].astype(jnp.bfloat16)
    gate_logit = mixed[..., 3 * channels :]
    wide_kv = with_halo(key_value, (("atoms", 1),), key_span)
    flat_grad = grad_out.reshape(sample_count * atom_count, channels)
    grad_y = jnp.dot(flat_grad, w_out.T, preferred_element_type=jnp.float32).reshape(
        sample_count, atom_count, channels
    )

    def one_sample(bias_sum, inputs):
        sample_query, sample_kv, sample_gate, sample_grad_y = inputs
        windowed = sample_kv[key_rows]
        gated, d_query, d_gate, d_keys, d_values, d_scores = attend(
            sample_query,
            windowed[..., :channels],
            windowed[..., channels:],
            sample_gate,
            sample_grad_y,
            pair_bias,
            key_live,
        )
        d_windowed = jnp.concatenate(
            [
                d_keys.reshape(windows, key_span, channels),
                d_values.reshape(windows, key_span, channels),
            ],
            axis=-1,
        )
        d_wide = jnp.zeros(sample_kv.shape, jnp.float32).at[key_rows].add(d_windowed)
        return (bias_sum + d_scores, (gated, d_query, d_gate, d_wide))

    bias_local, (gated, d_query, d_gate, d_wide) = lax.scan(
        one_sample, jnp.zeros(pair_bias.shape, jnp.float32), (query, wide_kv, gate_logit, grad_y)
    )
    inner_grad = d_wide[:, key_span : key_span + atom_count]
    from_upper = passed_along(d_wide[:, :key_span].astype(jnp.bfloat16), "atoms", -1).astype(
        jnp.float32
    )
    from_lower = passed_along(
        d_wide[:, key_span + atom_count :].astype(jnp.bfloat16), "atoms", 1
    ).astype(jnp.float32)
    kv_grad = (
        inner_grad.at[:, :key_span].add(from_lower).at[:, atom_count - key_span :].add(from_upper)
    )
    kv_rounded = kv_grad.astype(jnp.bfloat16)
    stacked = jnp.concatenate([d_query, kv_rounded, d_gate], axis=-1).reshape(
        sample_count * atom_count, 4 * channels
    )
    grad_act = (
        jnp.dot(stacked, projection.T, preferred_element_type=jnp.float32)
        .astype(jnp.bfloat16)
        .reshape(sample_count, atom_count, channels)
    )
    weight_part = jnp.dot(flat_act.T, stacked, preferred_element_type=jnp.float32)
    out_part = jnp.dot(gated.reshape(-1, channels).T, flat_grad, preferred_element_type=jnp.float32)
    pair_weight_part = jnp.einsum(
        "wicj,whij->ch", pair, bias_local, preferred_element_type=jnp.float32
    )
    token_part = jnp.sum(jnp.where(same_token[:, None, :, :], bias_local, 0.0), axis=(0, 2, 3))
    weight_sum, out_sum, grad_pair_weight, grad_token_weight = lax.psum(
        (weight_part, out_part, pair_weight_part, token_part), ("atoms", "samples")
    )
    grad_weights = jnp.concatenate(
        [weight_sum.reshape(channels, 4, channels).transpose(1, 0, 2), out_sum[None]], axis=0
    )
    sample_ways = lax.axis_size("samples")
    share_rows = win_rows // sample_ways
    bias_total = lax.psum(bias_local.astype(jnp.bfloat16), "samples").astype(jnp.float32)
    my_share = lax.dynamic_slice_in_dim(
        bias_total, lax.axis_index("samples") * share_rows, share_rows, 2
    )
    grad_pair = jnp.einsum(
        "whij,ch->wicj", my_share, w_pair.astype(jnp.float32), precision=lax.Precision.HIGHEST
    ).astype(jnp.bfloat16)
    return (grad_act, grad_pair, grad_weights, grad_pair_weight, grad_token_weight)


def solution(mesh):
    in_specs = (
        P("samples", ("groups", "atoms"), None),
        P("samples", ("groups", "atoms"), None),
        P(("groups", "atoms"), None, None, None),
        P(),
        P(),
        P(),
        P(),
        P(),
        P(),
        P(),
        P(("groups", "atoms")),
        P(("groups", "atoms")),
        P(("groups", "atoms")),
    )
    out_specs = (
        P("samples", ("groups", "atoms"), None),
        P(("groups", "atoms"), "samples", None, None),
        P("groups", None, None),
        P("groups", None),
        P("groups"),
    )
    return jax.shard_map(
        per_device, mesh=mesh, in_specs=in_specs, out_specs=out_specs, check_vma=False
    )
```

profile of v0, /device:TPU:8, one launch (start us, length us, event | category | flops | bytes accessed | tf_op | source)
XLA Modules:
  0.0 949.7 jit_solution(12060509717389246733)
XLA Ops:
  11.1 6.7 convolution_bitcast_fusion.1
  17.8 11.4 %copy.63 = f32[5120,512]{1,0:T(8,128)} copy(f32[5120,512]{0,1:T(8,128)} %convolution_bitcast_fusion.1) | data formatting | bytes 20971520 | tf_op jit(solution)/shard_map/reshape | solution.py:118
  29.2 4.7 convert.8
  35.1 3.4 collective-permute-start.2
  38.4 3.3 collective-permute-start.3
  45.0 4.2 collective-permute-start.1
  50.6 3.4 slice.115
  57.5 3.7 collective-permute-done
  63.1 9.4 gather_fusion.1
  78.5 686.5 %while.21 = (s32[]{:T(128)}, f32[20,4,32,128]{3,2,1,0:T(8,128)}, bf16[8,640,128]{2,1,0:T(8,128)(2,1)}, bf16[8,640,128]{1,2,0:T(8,128)(2,1)}, bf16[8,640,128]{1,2...) while((s32[]{:T(128)}, f32[20,4,32,128]{3,2,1,0:T(8,128)}, ...), condition=%wide.region_5.6_spmd.clone, body=%wide.region_0.5_spmd.clone.sunk | while | flops 135430016 | bytes 73126840 | solution.py:152
  79.6 8.1 gather_fusion
  99.7 7.5 convolution_bitcast_fusion.5
  116.8 7.5 fusion.113
  124.3 3.3 multiply_reduce_fusion.2
  137.1 15.7 %scatter_custom_fusion.6 = f32[896,256]{1,0:T(8,128)} fusion(s32[2560]{0:T(1024)S(1)} %fusion.106, f32[2560,256]{1,0:T(8,128)} %bitcast.143, f32[]{:T(128)} %constant.105.clone.5..sunk), kind=kCustom, calls=%fused_computation.21.clone.1 | custom fusion | flops 655360 | bytes 918016 | tf_op jit(solution)/shard_map/while/body/eval_jaxpr/scatter-add | solution.py:149
  165.1 8.1 gather_fusion
  185.2 7.5 convolution_bitcast_fusion.5
  202.3 7.5 fusion.113
  209.8 3.3 multiply_reduce_fusion.2
  213.1 3.4 fusion.110
  219.6 3.3 copy.101
  222.9 15.7 %scatter_custom_fusion.6 = f32[896,256]{1,0:T(8,128)} fusion(s32[2560]{0:T(1024)S(1)} %fusion.106, f32[2560,256]{1,0:T(8,128)} %bitcast.143, f32[]{:T(128)} %constant.105.clone.5..sunk), kind=kCustom, calls=%fused_computation.21.clone.1 | custom fusion | flops 655360 | bytes 918016 | tf_op jit(solution)/shard_map/while/body/eval_jaxpr/scatter-add | solution.py:149
  251.0 8.1 gather_fusion
  271.1 7.5 convolution_bitcast_fusion.5
  288.2 7.5 fusion.113
  295.7 3.3 multiply_reduce_fusion.2
  299.0 3.4 fusion.110
  308.8 15.7 %scatter_custom_fusion.6 = f32[896,256]{1,0:T(8,128)} fusion(s32[2560]{0:T(1024)S(1)} %fusion.106, f32[2560,256]{1,0:T(8,128)} %bitcast.143, f32[]{:T(128)} %constant.105.clone.5..sunk), kind=kCustom, calls=%fused_computation.21.clone.1 | custom fusion | flops 655360 | bytes 918016 | tf_op jit(solution)/shard_map/while/body/eval_jaxpr/scatter-add | solution.py:149
  336.8 8.1 gather_fusion
  356.9 7.5 convolution_bitcast_fusion.5
  374.0 7.5 fusion.113
  384.9 3.4 fusion.110
  391.3 3.3 copy.101
  394.6 15.7 %scatter_custom_fusion.6 = f32[896,256]{1,0:T(8,128)} fusion(s32[2560]{0:T(1024)S(1)} %fusion.106, f32[2560,256]{1,0:T(8,128)} %bitcast.143, f32[]{:T(128)} %constant.105.clone.5..sunk), kind=kCustom, calls=%fused_computation.21.clone.1 | custom fusion | flops 655360 | bytes 918016 | tf_op jit(solution)/shard_map/while/body/eval_jaxpr/scatter-add | solution.py:149
  422.7 8.1 gather_fusion
  442.8 7.5 convolution_bitcast_fusion.5
  459.9 7.5 fusion.113
  470.7 3.4 fusion.110
  477.1 3.3 copy.101
  480.5 15.7 %scatter_custom_fusion.6 = f32[896,256]{1,0:T(8,128)} fusion(s32[2560]{0:T(1024)S(1)} %fusion.106, f32[2560,256]{1,0:T(8,128)} %bitcast.143, f32[]{:T(128)} %constant.105.clone.5..sunk), kind=kCustom, calls=%fused_computation.21.clone.1 | custom fusion | flops 655360 | bytes 918016 | tf_op jit(solution)/shard_map/while/body/eval_jaxpr/scatter-add | solution.py:149
  508.5 8.1 gather_fusion
  528.6 7.5 convolution_bitcast_fusion.5
  545.7 7.5 fusion.113
  553.2 3.3 multiply_reduce_fusion.2
  556.6 3.4 fusion.110
  566.3 15.7 %scatter_custom_fusion.6 = f32[896,256]{1,0:T(8,128)} fusion(s32[2560]{0:T(1024)S(1)} %fusion.106, f32[2560,256]{1,0:T(8,128)} %bitcast.143, f32[]{:T(128)} %constant.105.clone.5..sunk), kind=kCustom, calls=%fused_computation.21.clone.1 | custom fusion | flops 655360 | bytes 918016 | tf_op jit(solution)/shard_map/while/body/eval_jaxpr/scatter-add | solution.py:149
  594.4 8.1 gather_fusion
  614.5 7.5 convolution_bitcast_fusion.5
  631.6 7.5 fusion.113
  642.4 3.4 fusion.110
  648.9 3.3 copy.101
  652.2 15.7 %scatter_custom_fusion.6 = f32[896,256]{1,0:T(8,128)} fusion(s32[2560]{0:T(1024)S(1)} %fusion.106, f32[2560,256]{1,0:T(8,128)} %bitcast.143, f32[]{:T(128)} %constant.105.clone.5..sunk), kind=kCustom, calls=%fused_computation.21.clone.1 | custom fusion | flops 655360 | bytes 918016 | tf_op jit(solution)/shard_map/while/body/eval_jaxpr/scatter-add | solution.py:149
  680.3 8.1 gather_fusion
  700.4 7.5 convolution_bitcast_fusion.5
  717.5 7.5 fusion.113
  728.3 3.4 fusion.110
  738.1 15.7 %scatter_custom_fusion.6 = f32[896,256]{1,0:T(8,128)} fusion(s32[2560]{0:T(1024)S(1)} %fusion.106, f32[2560,256]{1,0:T(8,128)} %bitcast.143, f32[]{:T(128)} %constant.105.clone.5..sunk), kind=kCustom, calls=%fused_computation.21.clone.1 | custom fusion | flops 655360 | bytes 918016 | tf_op jit(solution)/shard_map/while/body/eval_jaxpr/scatter-add | solution.py:149
  765.0 3.8 convert.9
  778.6 4.2 collective-permute-start.5
  784.5 30.8 %all-reduce = (f32[16,4]{0,1:T(4,128)}, f32[4]{0:T(128)}) all-reduce(f32[16,4]{0,1:T(4,128)S(1)} %fusion.22, f32[4]{0:T(128)S(1)} %select_reduce_fusion), channel_id=1, replica_groups=mesh['groups'=2,'atoms'=8,'samples'=2] {'atoms','samples'}, use_global_device_ids=true, to_apply=%region_9.10 | all-reduce | flops 68 | bytes 544 | tf_op jit(solution)/shard_map/psum | solution.py:180
  829.2 7.8 copy.54
  837.1 4.4 fusion.42
  842.3 5.1 convolution_convert_fusion
  850.1 91.1 %all-reduce.7.cloned.1.call-done = (f32[1,128,128]{2,1,0:T(8,128)}, f32[4,128,128]{2,1,0:T(8,128)}) async-done(((f32[1,128,128]{2,1,0:T(8,128)}, f32[4,128,128]{2,1,0:T(8,128)}), (f32[1,128,128]{2,1,0:T(8,128)}, f32[4,128,128]{2,1,0:T(8,128)})) %all-reduce.7.cloned.1.call-update) | async-done | bytes 327696 | tf_op jit(solution)/shard_map/psum | solution.py:180
  (406 shorter events, 375.3 us)
Async XLA Ops:
  7.2 65.5 %copy-start = (bf16[20,32,16,128]{3,2,1,0:T(8,128)(2,1)S(1)}, bf16[20,32,16,128]{3,2,1,0:T(8,128)(2,1)}, u32[]{:S(2)}) copy-start(bf16[20,32,16,128]{3,2,1,0:T(8,128)(2,1)} %param.21) | copy-start | bytes 7864324
  7.2 840.3 %all-reduce.5.cloned.1.call-start = ((), (), s32[]{:S(2)}) async-start(), calls=%async_computation | async-start | bytes 1310720 | tf_op jit(solution)/shard_map/psum | solution.py:188
  33.9 15.4 %copy-start.9 = (bf16[8,640,512]{2,1,0:T(8,128)(2,1)}, bf16[8,640,512]{2,1,0:T(8,128)(2,1)S(1)}, u32[]{:S(2)}) copy-start(bf16[8,640,512]{2,1,0:T(8,128)(2,1)S(1)} %convert.8) | copy-start | bytes 15728644
  33.9 8.6 copy-start.16
  35.1 39.5 %collective-permute-start.2 = (bf16[8,128,256]{2,1,0:T(8,128)(2,1)}, bf16[8,128,256]{2,1,0:T(8,128)(2,1)S(1)}, u32[]{:S(2)}, u32[]{:S(2)}) collective-permute-start(bf16[8,128,256]{2,1,0:T(8,128)(2,1)} %get-tuple-element.218), channel_id=1, source_target_pairs={{0,2},{2,4},{4,6},{6,8},{8,10},{10,12},{12,14},{1,3},{3,5},{5,7},{... | collective-permute-start | bytes 1572872 | tf_op jit(solution)/shard_map/ppermute | solution.py:17
  38.4 36.1 %collective-permute-start.3 = (bf16[8,128,256]{2,1,0:T(8,128)(2,1)}, bf16[8,128,256]{2,1,0:T(8,128)(2,1)}, u32[]{:S(2)}, u32[]{:S(2)}) collective-permute-start(bf16[8,128,256]{2,1,0:T(8,128)(2,1)} %get-tuple-element.219), channel_id=1, source_target_pairs={{2,0},{4,2},{6,4},{8,6},{10,8},{12,10},{14,12},{3,1},{5,3},{7,5},{... | collective-permute-start | bytes 1572872 | tf_op jit(solution)/shard_map/ppermute | solution.py:18
  42.5 18.7 %collective-permute-start = (s32[128]{0:T(128)S(1)}, s32[128]{0:T(128)S(1)}, u32[]{:S(2)}, u32[]{:S(2)}) collective-permute-start(s32[128]{0:T(128)S(1)} %get-tuple-element.226), channel_id=1, source_target_pairs={{0,2},{2,4},{4,6},{6,8},{8,10},{10,12},{12,14},{1,3},{3,5},{5,7},{... | collective-permute-start | bytes 1544 | tf_op jit(solution)/shard_map/ppermute | solution.py:17
  45.0 18.1 %collective-permute-start.1 = (s32[128]{0:T(128)S(1)}, s32[128]{0:T(128)S(1)}, u32[]{:S(2)}, u32[]{:S(2)}) collective-permute-start(s32[128]{0:T(128)S(1)} %get-tuple-element.227), channel_id=1, source_target_pairs={{2,0},{4,2},{6,4},{8,6},{10,8},{12,10},{14,12},{3,1},{5,3},{7,5},{... | collective-permute-start | bytes 1544 | tf_op jit(solution)/shard_map/ppermute | solution.py:18
  50.6 3.5 copy-start.19
  50.6 3.6 copy-start.15
  63.1 9.6 %copy-start.17 = (bf16[16,4]{0,1:T(4,128)(2,1)S(1)}, bf16[16,4]{0,1:T(4,128)(2,1)}, u32[]{:S(2)}) copy-start(bf16[16,4]{0,1:T(4,128)(2,1)} %param.27) | copy-start | bytes 388
  63.1 9.6 %copy-start.18 = (f32[4]{0:T(128)S(1)}, f32[4]{0:T(128)}, u32[]{:S(2)}) copy-start(f32[4]{0:T(128)} %param.28) | copy-start | bytes 52
  73.3 2.2 slice-start
  94.6 2.2 copy-start.1
  99.7 7.5 copy-start.10
  111.6 5.2 copy-start.5
  127.6 3.1 copy-start.2
  155.1 2.2 copy-start.3
  180.0 2.2 copy-start.1
  185.2 7.5 copy-start.10
  197.1 5.2 copy-start.5
  213.1 3.4 copy-start.2
  241.0 2.3 copy-start.3
  265.9 2.2 copy-start.1
  271.1 7.5 copy-start.10
  283.0 5.2 copy-start.5
  299.0 3.4 copy-start.2
  326.8 2.2 copy-start.3
  351.8 2.2 copy-start.1
  354.0 1.6 copy-start.4
  356.9 7.5 copy-start.10
  368.8 5.2 copy-start.5
  384.9 3.4 copy-start.2
  412.7 2.2 copy-start.3
  437.6 2.2 copy-start.1
  442.8 7.5 copy-start.10
  454.7 5.2 copy-start.5
  470.7 3.4 copy-start.2
  498.5 2.2 copy-start.3
  523.5 2.2 copy-start.1
  525.6 1.6 copy-start.4
  528.6 7.5 copy-start.10
  540.5 5.2 copy-start.5
  556.6 3.4 copy-start.2
  584.4 2.3 copy-start.3
  609.4 2.2 copy-start.1
  611.5 1.6 copy-start.4
  614.5 7.5 copy-start.10
  626.4 5.2 copy-start.5
  642.4 3.4 copy-start.2
  670.3 2.2 copy-start.3
  695.2 2.2 copy-start.1
  700.4 7.5 copy-start.10
  712.3 5.2 copy-start.5
  728.3 3.4 copy-start.2
  756.1 2.2 copy-start.3
  765.0 9.1 copy-start.8
  768.8 3.8 copy-start.6
  770.0 48.2 %collective-permute-start.4 = (bf16[8,128,256]{1,2,0:T(8,128)(2,1)}, bf16[8,128,256]{1,2,0:T(8,128)(2,1)S(1)}, u32[]{:S(2)}, u32[]{:S(2)}) collective-permute-start(bf16[8,128,256]{1,2,0:T(8,128)(2,1)} %get-tuple-element.221), channel_id=1, source_target_pairs={{0,2},{2,4},{4,6},{6,8},{8,10},{10,12},{12,14},{1,3},{3,5},{5,7},{... | collective-permute-start | bytes 1572872 | tf_op jit(solution)/shard_map/ppermute | solution.py:26
  778.6 42.0 %collective-permute-start.5 = (bf16[8,128,256]{1,2,0:T(8,128)(2,1)}, bf16[8,128,256]{1,2,0:T(8,128)(2,1)}, u32[]{:S(2)}, u32[]{:S(2)}) collective-permute-start(bf16[8,128,256]{1,2,0:T(8,128)(2,1)} %get-tuple-element.220), channel_id=1, source_target_pairs={{2,0},{4,2},{6,4},{8,6},{10,8},{12,10},{14,12},{3,1},{5,3},{7,5},{... | collective-permute-start | bytes 1572872 | tf_op jit(solution)/shard_map/ppermute | solution.py:26
  782.9 158.3 %all-reduce.7.cloned.1.call-start = ((), (), s32[]{:S(2)}) async-start(), calls=%async_computation.1 | async-start | bytes 655360 | tf_op jit(solution)/shard_map/psum | solution.py:180
  823.2 2.9 copy-start.11
  823.2 3.3 copy-start.12
  837.1 5.3 copy-start.14
  (14 other events, 19.0 us)
Sparse Core Ops, SparseCore 0:
  783.0 19.4 all-reduce.4
  847.6 93.5 all-reduce.6
where the time goes:
time: 956 us; the launch traced here: 950 us
  local copies, waits for them, and re-layouts  353 us (37%)
  other arithmetic  235 us (25%)
  matrix products  198 us (21%)
  waiting for transfers between devices  96.7 us (10%)
  blocking collectives  30.8 us (3%)
  starting transfers between devices  20.3 us (2%)
  between operations  15 us (2%)
    scatter-add x8, other arithmetic, one_sample(): jnp.zeros(sample_kv.shape, jnp.float32).at[key_rows].add(d_windowed)  125 us
    psum x1, waiting for transfers between devices, per_device(): lax.psum((weight_part, out_part, pair_weight_part, token_part), ('atoms',...  91.1 us
    dynamic_update_slice x48, local copies, waits for them, and re-layouts, per_device(): lax.scan(one_sample, jnp.zeros(pair_bias.shape, jnp.float32), (query, wid...  71.6 us
    gather x8, local copies, waits for them, and re-layouts, one_sample(): windowed = sample_kv[key_rows]  65.1 us
    dot_general x8, matrix products, attend(): jnp.einsum('whij,wjhd->wihd', probs_b, value_heads, preferred_element_typ...  60.3 us
    dot_general x8, matrix products, attend(): jnp.einsum('whij,wihd->wjhd', probs_b, attended_heads, preferred_element_...  59.8 us
    psum x1, blocking collectives, per_device(): lax.psum((weight_part, out_part, pair_weight_part, token_part), ('atoms',...  30.8 us
    while x128, local copies, waits for them, and re-layouts  28 us
  transfers between devices with their start and end apart: 8, of which 3 were waited for; matrix products, arithmetic and copies ran while one was open for 6% of the time, Pallas kernels for 0%

commit v1 on v0

--- a/solution.py
+++ b/solution.py
@@ -178,7 +178,7 @@
     )
     token_part = jnp.sum(jnp.where(same_token[:, None, :, :], bias_local, 0.0), axis=(0, 2, 3))
     weight_sum, out_sum, grad_pair_weight, grad_token_weight = lax.psum(
-        (weight_part, out_part, pair_weight_part, token_part), ("atoms", "samples")
+        lax.psum((weight_part, out_part, pair_weight_part, token_part), "samples"), "atoms"
     )
     grad_weights = jnp.concatenate(
         [weight_sum.reshape(channels, 4, channels).transpose(1, 0, 2), out_sum[None]], axis=0

time: 956 us -> 937 us (0.980)
  blocking collectives: 30.8 us -> 19.9 us
    psum x1 -> x2, waiting for transfers between devices: 91.1 us -> 67.9 us  [the longest x1 67.9 us: per_device(): lax.psum(lax.psum((weight_part, out_part, pair_weight_part, token_part),...]
    ppermute x2, waiting for transfers between devices: 0.01 us -> 19.4 us  [passed_along(): lax.ppermute(value, axis, [(source, source + steps) for source in range(i...]
    psum x1 -> x2, blocking collectives: 30.8 us -> 19.9 us  [the longest x1 17.4 us: per_device(): lax.psum(lax.psum((weight_part, out_part, pair_weight_part, token_part),...]
  transfers between devices with their start and end apart: 8 -> 9, of which waited for: 3 -> 5; matrix products, arithmetic and copies ran while one was open for 6% -> 5% of each run, Pallas kernels for 0% -> 0%
where the time goes in v1:
time: 937 us; the launch traced here: 929 us
  local copies, waits for them, and re-layouts  355 us (38%)
  other arithmetic  231 us (25%)
  matrix products  194 us (21%)
  waiting for transfers between devices  93 us (10%)
  starting transfers between devices  20.6 us (2%)
  blocking collectives  19.9 us (2%)
  between operations  14.8 us (2%)
    scatter-add x8, other arithmetic, one_sample(): jnp.zeros(sample_kv.shape, jnp.float32).at[key_rows].add(d_windowed)  125 us
    dynamic_update_slice x48, local copies, waits for them, and re-layouts, per_device(): lax.scan(one_sample, jnp.zeros(pair_bias.shape, jnp.float32), (query, wid...  71.6 us
    psum x1, waiting for transfers between devices, per_device(): lax.psum(lax.psum((weight_part, out_part, pair_weight_part, token_part),...  67.9 us
    gather x8, local copies, waits for them, and re-layouts, one_sample(): windowed = sample_kv[key_rows]  65.2 us
    dot_general x8, matrix products, attend(): jnp.einsum('whij,wjhd->wihd', probs_b, value_heads, preferred_element_typ...  60.5 us
    dot_general x8, matrix products, attend(): jnp.einsum('whij,wihd->wjhd', probs_b, attended_heads, preferred_element_...  60 us
    while x128, local copies, waits for them, and re-layouts  28 us
    convert_element_type x8, other arithmetic, attend(): ds_b = d_scores.astype(jnp.bfloat16)  27 us
  transfers between devices with their start and end apart: 9, of which 5 were waited for; matrix products, arithmetic and copies ran while one was open for 5% of the time, Pallas kernels for 0%

profile of v1, /device:TPU:8, one launch (start us, length us, event | category | flops | bytes accessed | tf_op | source)
XLA Modules:
  0.0 928.9 jit_solution(2196508342533310514)
XLA Ops:
  11.1 6.7 convolution_bitcast_fusion.1
  17.8 11.4 %copy.63 = f32[5120,512]{1,0:T(8,128)} copy(f32[5120,512]{0,1:T(8,128)} %convolution_bitcast_fusion.1) | data formatting | bytes 20971520 | tf_op jit(solution)/shard_map/reshape | solution.py:118
  29.2 4.7 convert.8
  35.1 3.4 collective-permute-start.2
  45.0 4.2 collective-permute-start.1
  54.0 3.4 slice.115
  57.5 3.7 collective-permute-done
  63.1 9.4 %gather_fusion.1 = s32[2560]{0:T(1024)S(1)} fusion(s32[896]{0:T(1024)S(1)} %pad_add_fusion, s32[3072]{0:T(1024)S(1)} %pad_clamp_fusion.1), kind=kCustom, calls=%fused_computation.1 | custom fusion | bytes 30720 | tf_op jit(solution)/shard_map/gather | solution.py:110
  78.5 687.0 %while.21 = (s32[]{:T(128)}, f32[20,4,32,128]{3,2,1,0:T(8,128)}, bf16[8,640,128]{2,1,0:T(8,128)(2,1)}, bf16[8,640,128]{1,2,0:T(8,128)(2,1)}, bf16[8,640,128]{1,2...) while((s32[]{:T(128)}, f32[20,4,32,128]{3,2,1,0:T(8,128)}, ...), condition=%wide.region_5.6_spmd.clone, body=%wide.region_0.5_spmd.clone.sunk | while | flops 135430016 | bytes 73126840 | solution.py:152
  79.6 8.1 gather_fusion
  99.7 7.6 convolution_bitcast_fusion.6
  116.9 7.5 fusion.111
  124.4 3.3 multiply_reduce_fusion.2
  137.1 15.7 %scatter_custom_fusion.6 = f32[896,256]{1,0:T(8,128)} fusion(s32[2560]{0:T(1024)S(1)} %fusion.104, f32[2560,256]{1,0:T(8,128)} %bitcast.142, f32[]{:T(128)} %constant.105.clone.5..sunk), kind=kCustom, calls=%fused_computation.21.clone.1 | custom fusion | flops 655360 | bytes 918016 | tf_op jit(solution)/shard_map/while/body/eval_jaxpr/scatter-add | solution.py:149
  165.2 8.1 gather_fusion
  185.3 7.6 convolution_bitcast_fusion.6
  202.4 7.5 fusion.111
  209.9 3.3 multiply_reduce_fusion.2
  213.3 3.4 fusion.108
  223.0 15.7 %scatter_custom_fusion.6 = f32[896,256]{1,0:T(8,128)} fusion(s32[2560]{0:T(1024)S(1)} %fusion.104, f32[2560,256]{1,0:T(8,128)} %bitcast.142, f32[]{:T(128)} %constant.105.clone.5..sunk), kind=kCustom, calls=%fused_computation.21.clone.1 | custom fusion | flops 655360 | bytes 918016 | tf_op jit(solution)/shard_map/while/body/eval_jaxpr/scatter-add | solution.py:149
  251.1 8.1 gather_fusion
  271.2 7.6 convolution_bitcast_fusion.6
  288.4 7.5 fusion.111
  295.9 3.3 multiply_reduce_fusion.2
  299.2 3.4 fusion.108
  309.0 15.7 %scatter_custom_fusion.6 = f32[896,256]{1,0:T(8,128)} fusion(s32[2560]{0:T(1024)S(1)} %fusion.104, f32[2560,256]{1,0:T(8,128)} %bitcast.142, f32[]{:T(128)} %constant.105.clone.5..sunk), kind=kCustom, calls=%fused_computation.21.clone.1 | custom fusion | flops 655360 | bytes 918016 | tf_op jit(solution)/shard_map/while/body/eval_jaxpr/scatter-add | solution.py:149
  337.0 8.1 gather_fusion
  357.1 7.6 convolution_bitcast_fusion.6
  374.3 7.5 fusion.111
  381.8 3.3 multiply_reduce_fusion.2
  385.1 3.4 fusion.108
  394.9 15.7 %scatter_custom_fusion.6 = f32[896,256]{1,0:T(8,128)} fusion(s32[2560]{0:T(1024)S(1)} %fusion.104, f32[2560,256]{1,0:T(8,128)} %bitcast.142, f32[]{:T(128)} %constant.105.clone.5..sunk), kind=kCustom, calls=%fused_computation.21.clone.1 | custom fusion | flops 655360 | bytes 918016 | tf_op jit(solution)/shard_map/while/body/eval_jaxpr/scatter-add | solution.py:149
  422.9 8.1 gather_fusion
  443.0 7.6 convolution_bitcast_fusion.6
  460.2 7.5 fusion.111
  467.7 3.3 multiply_reduce_fusion.2
  471.0 3.4 fusion.108
  480.8 15.7 %scatter_custom_fusion.6 = f32[896,256]{1,0:T(8,128)} fusion(s32[2560]{0:T(1024)S(1)} %fusion.104, f32[2560,256]{1,0:T(8,128)} %bitcast.142, f32[]{:T(128)} %constant.105.clone.5..sunk), kind=kCustom, calls=%fused_computation.21.clone.1 | custom fusion | flops 655360 | bytes 918016 | tf_op jit(solution)/shard_map/while/body/eval_jaxpr/scatter-add | solution.py:149
  508.8 8.1 gather_fusion
  528.9 7.6 convolution_bitcast_fusion.6
  546.1 7.5 fusion.111
  553.6 3.3 multiply_reduce_fusion.2
  556.9 3.4 fusion.108
  566.7 15.7 %scatter_custom_fusion.6 = f32[896,256]{1,0:T(8,128)} fusion(s32[2560]{0:T(1024)S(1)} %fusion.104, f32[2560,256]{1,0:T(8,128)} %bitcast.142, f32[]{:T(128)} %constant.105.clone.5..sunk), kind=kCustom, calls=%fused_computation.21.clone.1 | custom fusion | flops 655360 | bytes 918016 | tf_op jit(solution)/shard_map/while/body/eval_jaxpr/scatter-add | solution.py:149
  594.7 8.1 gather_fusion
  614.9 7.6 convolution_bitcast_fusion.6
  632.0 7.5 fusion.111
  639.5 3.3 multiply_reduce_fusion.2
  642.8 3.4 fusion.108
  652.6 15.7 %scatter_custom_fusion.6 = f32[896,256]{1,0:T(8,128)} fusion(s32[2560]{0:T(1024)S(1)} %fusion.104, f32[2560,256]{1,0:T(8,128)} %bitcast.142, f32[]{:T(128)} %constant.105.clone.5..sunk), kind=kCustom, calls=%fused_computation.21.clone.1 | custom fusion | flops 655360 | bytes 918016 | tf_op jit(solution)/shard_map/while/body/eval_jaxpr/scatter-add | solution.py:149
  680.7 8.1 gather_fusion
  700.8 7.6 convolution_bitcast_fusion.6
  717.9 7.5 fusion.111
  725.4 3.3 multiply_reduce_fusion.2
  728.8 3.4 fusion.108
  738.6 15.7 %scatter_custom_fusion.6 = f32[896,256]{1,0:T(8,128)} fusion(s32[2560]{0:T(1024)S(1)} %fusion.104, f32[2560,256]{1,0:T(8,128)} %bitcast.142, f32[]{:T(128)} %constant.105.clone.5..sunk), kind=kCustom, calls=%fused_computation.21.clone.1 | custom fusion | flops 655360 | bytes 918016 | tf_op jit(solution)/shard_map/while/body/eval_jaxpr/scatter-add | solution.py:149
  765.4 3.8 convert.9
  772.6 4.3 collective-permute-start.5
  778.1 16.5 %collective-permute-done.4 = bf16[8,128,256]{1,2,0:T(8,128)(2,1)S(1)} collective-permute-done((bf16[8,128,256]{1,2,0:T(8,128)(2,1)S(1)}, bf16[8,128,256]{1,2,0:T(8,128)(2,1)S(1)}, u32[]{:S(2)}, u32[]{:S(2)}) %collective-permute-start.4) | collective-permute-done | bytes 524320 | tf_op jit(solution)/shard_map/ppermute | solution.py:26
  812.2 17.4 %all-reduce = (f32[16,4]{0,1:T(4,128)}, f32[4]{0:T(128)}) all-reduce(f32[16,4]{0,1:T(4,128)S(1)} %get-tuple-element.206, f32[4]{0:T(128)S(1)} %get-tuple-element.207), channel_id=1, replica_groups=mesh['groups'=2,'atoms'=8,'samples'=2] {'atoms'}, use_global_device_ids=true, to_apply=%region_12.13 | all-reduce | flops 68 | bytes 544 | tf_op jit(solution)/shard_map/psum | solution.py:180
  829.7 5.6 pad_maximum_fusion.1
  835.3 7.9 copy.54
  845.0 5.1 convolution_convert_fusion
  852.7 67.9 %all-reduce.10.cloned.1.call-done = (f32[1,128,128]{2,1,0:T(8,128)}, f32[4,128,128]{2,1,0:T(8,128)}) async-done(((f32[1,128,128]{2,1,0:T(8,128)}, f32[4,128,128]{2,1,0:T(8,128)}), (f32[1,128,128]{2,1,0:T(8,128)}, f32[4,128,128]{2,1,0:T(8,128)})) %all-reduce.10.cloned.1.call-update) | async-done | bytes 327696 | tf_op jit(solution)/shard_map/psum | solution.py:180
  (418 shorter events, 376.3 us)
Async XLA Ops:
  7.2 65.5 %copy-start = (bf16[20,32,16,128]{3,2,1,0:T(8,128)(2,1)S(1)}, bf16[20,32,16,128]{3,2,1,0:T(8,128)(2,1)}, u32[]{:S(2)}) copy-start(bf16[20,32,16,128]{3,2,1,0:T(8,128)(2,1)} %param.21) | copy-start | bytes 7864324
  7.2 836.0 %all-reduce.12.cloned.1.call-start = ((), (), s32[]{:S(2)}) async-start(), calls=%async_computation.2 | async-start | bytes 655360 | tf_op jit(solution)/shard_map/psum | solution.py:181
  33.9 15.4 %copy-start.9 = (bf16[8,640,512]{2,1,0:T(8,128)(2,1)}, bf16[8,640,512]{2,1,0:T(8,128)(2,1)S(1)}, u32[]{:S(2)}) copy-start(bf16[8,640,512]{2,1,0:T(8,128)(2,1)S(1)} %convert.8) | copy-start | bytes 15728644
  33.9 8.6 copy-start.20
  35.1 39.5 %collective-permute-start.2 = (bf16[8,128,256]{2,1,0:T(8,128)(2,1)}, bf16[8,128,256]{2,1,0:T(8,128)(2,1)S(1)}, u32[]{:S(2)}, u32[]{:S(2)}) collective-permute-start(bf16[8,128,256]{2,1,0:T(8,128)(2,1)} %get-tuple-element.222), channel_id=1, source_target_pairs={{0,2},{2,4},{4,6},{6,8},{8,10},{10,12},{12,14},{1,3},{3,5},{5,7},{... | collective-permute-start | bytes 1572872 | tf_op jit(solution)/shard_map/ppermute | solution.py:17
  38.5 36.1 %collective-permute-start.3 = (bf16[8,128,256]{2,1,0:T(8,128)(2,1)}, bf16[8,128,256]{2,1,0:T(8,128)(2,1)}, u32[]{:S(2)}, u32[]{:S(2)}) collective-permute-start(bf16[8,128,256]{2,1,0:T(8,128)(2,1)} %get-tuple-element.223), channel_id=1, source_target_pairs={{2,0},{4,2},{6,4},{8,6},{10,8},{12,10},{14,12},{3,1},{5,3},{7,5},{... | collective-permute-start | bytes 1572872 | tf_op jit(solution)/shard_map/ppermute | solution.py:18
  42.5 18.7 %collective-permute-start = (s32[128]{0:T(128)S(1)}, s32[128]{0:T(128)S(1)}, u32[]{:S(2)}, u32[]{:S(2)}) collective-permute-start(s32[128]{0:T(128)S(1)} %get-tuple-element.230), channel_id=1, source_target_pairs={{0,2},{2,4},{4,6},{6,8},{8,10},{10,12},{12,14},{1,3},{3,5},{5,7},{... | collective-permute-start | bytes 1544 | tf_op jit(solution)/shard_map/ppermute | solution.py:17
  45.0 18.1 %collective-permute-start.1 = (s32[128]{0:T(128)S(1)}, s32[128]{0:T(128)S(1)}, u32[]{:S(2)}, u32[]{:S(2)}) collective-permute-start(s32[128]{0:T(128)S(1)} %get-tuple-element.231), channel_id=1, source_target_pairs={{2,0},{4,2},{6,4},{8,6},{10,8},{12,10},{14,12},{3,1},{5,3},{7,5},{... | collective-permute-start | bytes 1544 | tf_op jit(solution)/shard_map/ppermute | solution.py:18
  63.1 9.6 %copy-start.21 = (bf16[16,4]{0,1:T(4,128)(2,1)S(1)}, bf16[16,4]{0,1:T(4,128)(2,1)}, u32[]{:S(2)}) copy-start(bf16[16,4]{0,1:T(4,128)(2,1)} %param.27) | copy-start | bytes 388
  63.1 9.6 %copy-start.22 = (f32[4]{0:T(128)S(1)}, f32[4]{0:T(128)}, u32[]{:S(2)}) copy-start(f32[4]{0:T(128)} %param.28) | copy-start | bytes 52
  73.3 2.2 slice-start
  94.6 2.2 copy-start.1
  99.7 7.6 copy-start.10
  111.6 5.2 copy-start.5
  127.7 3.1 copy-start.2
  155.2 2.2 copy-start.3
  180.1 2.2 copy-start.1
  185.3 7.6 copy-start.10
  197.2 5.2 copy-start.5
  213.3 3.4 copy-start.2
  241.1 2.3 copy-start.3
  266.1 2.2 copy-start.1
  271.2 7.6 copy-start.10
  283.1 5.2 copy-start.5
  299.2 3.4 copy-start.2
  327.1 2.2 copy-start.3
  352.0 2.2 copy-start.1
  354.2 1.5 copy-start.4
  357.1 7.6 copy-start.10
  369.0 5.2 copy-start.5
  385.1 3.4 copy-start.2
  412.9 2.2 copy-start.3
  437.9 2.2 copy-start.1
  443.0 7.6 copy-start.10
  454.9 5.2 copy-start.5
  471.0 3.4 copy-start.2
  498.8 2.2 copy-start.3
  523.8 2.2 copy-start.1
  528.9 7.6 copy-start.10
  540.8 5.2 copy-start.5
  556.9 3.4 copy-start.2
  584.7 2.2 copy-start.3
  609.7 2.2 copy-start.1
  614.8 7.6 copy-start.10
  626.8 5.2 copy-start.5
  642.8 3.4 copy-start.2
  670.7 2.3 copy-start.3
  695.6 2.2 copy-start.1
  700.8 7.6 copy-start.10
  712.7 5.2 copy-start.5
  728.8 3.4 copy-start.2
  756.6 2.2 copy-start.3
  765.4 6.8 copy-start.8
  769.5 7.4 copy-start.12
  769.5 7.4 copy-start.16
  769.5 25.0 %collective-permute-start.4 = (bf16[8,128,256]{1,2,0:T(8,128)(2,1)S(1)}, bf16[8,128,256]{1,2,0:T(8,128)(2,1)S(1)}, u32[]{:S(2)}, u32[]{:S(2)}) collective-permute-start(bf16[8,128,256]{1,2,0:T(8,128)(2,1)S(1)} %get-tuple-element.225), channel_id=1, source_target_pairs={{0,2},{2,4},{4,6},{6,8},{8,10},{10,12},{12,14},{1,3},{3,5},{5,7},{... | collective-permute-start | bytes 1572872 | tf_op jit(solution)/shard_map/ppermute | solution.py:26
  772.6 25.0 %collective-permute-start.5 = (bf16[8,128,256]{1,2,0:T(8,128)(2,1)S(1)}, bf16[8,128,256]{1,2,0:T(8,128)(2,1)S(1)}, u32[]{:S(2)}, u32[]{:S(2)}) collective-permute-start(bf16[8,128,256]{1,2,0:T(8,128)(2,1)S(1)} %get-tuple-element.224), channel_id=1, source_target_pairs={{2,0},{4,2},{6,4},{8,6},{10,8},{12,10},{14,12},{3,1},{5,3},{7,5},{... | collective-permute-start | bytes 1572872 | tf_op jit(solution)/shard_map/ppermute | solution.py:26
  797.9 1.8 copy-start.13
  797.9 2.6 copy-start.14
  797.9 3.0 copy-start.15
  803.2 46.9 %all-reduce.8.cloned.1.call-start = ((), (), s32[]{:S(2)}) async-start(), calls=%async_computation | async-start | bytes 1310720 | tf_op jit(solution)/shard_map/psum | solution.py:188
  806.4 114.2 %all-reduce.10.cloned.1.call-start = ((), (), s32[]{:S(2)}) async-start(), calls=%async_computation.1 | async-start | bytes 655360 | tf_op jit(solution)/shard_map/psum | solution.py:180
  806.5 1.7 copy-start.6
  835.3 9.7 %copy-start.18 = (bf16[128,512]{1,0:T(8,128)(2,1)S(1)}, bf16[128,512]{1,0:T(8,128)(2,1)}, u32[]{:S(2)}) copy-start(bf16[128,512]{1,0:T(8,128)(2,1)} %copy-done.17) | copy-start | bytes 393220
  (19 other events, 26.3 us)
Sparse Core Ops, SparseCore 0:
  803.3 18.8 all-reduce.11
  824.7 20.1 all-reduce.7
  848.9 71.6 all-reduce.9
